TPU v7x, 32 devices: a whole 2x2x4 slice. The times are simulated.
32 devices in a mesh: bfly: 32 (over z, y, x, core).
Axes of the slice: x: 2, y: 2, z: 4, core: 2. Of those that a mesh axis runs over, the one named last changes fastest.
Arguments:
- coeffs: float32 [32, 384, 1024], P('bfly'), may hold values from -6 to 6
- transfers: float32 [32, 8, 2, 384, 384], P('bfly'), may hold values from -0.21875 to 0.21875
Outputs:
- result: float32 [32, 384, 1024], P('bfly')
All inputs are finite; a program needn't handle non-finite values.
Results may differ from a plain program's by a relative error of at most 0.00014.
Values sent between devices are 32-bit elements; how exact they have to be, the bound alone decides.
A program may use at most 64 MiB of HBM per device.

v0:
```python
import functools

import jax
import jax.numpy as jnp
from jax import lax
from jax.experimental import pallas as pl
from jax.experimental.pallas import tpu as pltpu
from jax.sharding import PartitionSpec as P

LANES = 128
CHUNK = 64
RAMP = (32, 32)
DUE = (0.0, 2.1, 6.5, 11.9, 17.4, 24.8, 25.6, 33.5, 44.4)
PACE = 0.066
GROUP = 9


def chunk_runs(cols):
    body = cols - 2 * sum(RAMP)
    sizes = (CHUNK,) * (cols // CHUNK)
    if body > 0 and body % CHUNK == 0:
        sizes = RAMP + (CHUNK,) * (body // CHUNK) + RAMP[::-1]
    runs = []
    for k, size in enumerate(sizes):
        if not runs or runs[-1][2] != size:
            runs.append((k, sum(sizes[:k]), size))
    return runs, sizes


def task_order(sizes, levels):
    dues = [DUE[i] if i < len(DUE) else DUE[-1] + 6.0 * (i - len(DUE) + 1) for i in range(levels + 1)]
    steps = sorted(
        (sum(sizes[:k]) * PACE + dues[level], -level, level, k)
        for k in range(len(sizes)) for level in range(levels + 1)
    )
    return [(level, k) for _, _, level, k in steps]


def kernel(axis, bits, levels, coeffs, transfers, out, own, sent, got, raw, mats, turn, back,
           in_sem, raw_sem, out_sem, send_sem, recv_sem):
    me = lax.axis_index(axis)
    cols, rank = own.shape
    blocks = cols // LANES
    runs, sizes = chunk_runs(cols)
    order = task_order(sizes, levels)
    base = max(levels + 1, len(sizes))

    def peer(level):
        step = lax.shift_left(jnp.int32(1), lax.rem(jnp.int32(level), jnp.int32(bits)))
        return me + step * (1 - 2 * lax.rem(lax.div(me, step), jnp.int32(2)))

    def lanes(b):
        return pl.ds(pl.multiple_of(b * LANES, LANES), LANES)

    def load_block(b):
        return pltpu.make_async_copy(coeffs.at[0, :, lanes(b)], turn.at[b], in_sem.at[b])

    def load_level(level):
        return pltpu.make_async_copy(transfers.at[0, level], raw.at[level], raw_sem.at[level])

    def store_block(b):
        return pltpu.make_async_copy(back.at[b], out.at[0, :, lanes(b)], out_sem.at[b])

    def exchange(level, k, rows):
        return pltpu.make_async_remote_copy(
            src_ref=sent.at[level, rows],
            dst_ref=got.at[level + 1, rows],
            send_sem=send_sem.at[level],
            recv_sem=recv_sem.at[level, k],
            device_id=(peer(level),),
            device_id_type=pl.DeviceIdType.MESH,
        )

    barrier = pltpu.get_barrier_semaphore()
    for bit in range(min(bits, levels)):
        pl.semaphore_signal(barrier, inc=1, device_id=(peer(bit),),
                            device_id_type=pl.DeviceIdType.MESH)

    load_block(0).start()
    for level in range(levels):
        load_level(level).start()
        if level == 0:
            for b in range(1, blocks):
                load_block(b).start()

    def prepare(level):
        load_level(level).wait()
        for side in range(2):
            full = raw[level, side].T
            high = full.astype(jnp.bfloat16)
            low = (full - high.astype(jnp.float32)).astype(jnp.bfloat16)
            mats[level, 0:rank, side * rank:(side + 1) * rank] = high
            mats[level, rank:2 * rank, side * rank:(side + 1) * rank] = low

    def turn_block(b):
        load_block(b).wait()
        rows = pl.ds(pl.multiple_of(b * LANES, LANES), LANES)
        own[rows] = turn[b].T
        got[0, rows] = jnp.zeros((LANES, rank), jnp.float32)

    def apply(size, level, k, row):
        rows = pl.ds(pl.multiple_of(row, 16), size)

        @pl.when(k == 0)
        def _():
            prepare(level)

        @pl.when((level == 0) & (lax.rem(row, LANES) == 0))
        def _():
            turn_block(lax.div(row, LANES))

        @pl.when(level > 0)
        def _():
            exchange(level - 1, k, rows).wait_recv()

        state = own[rows] + got[level, rows]
        high = state.astype(jnp.bfloat16)
        low = (state - high.astype(jnp.float32)).astype(jnp.bfloat16)
        both = jnp.dot(jnp.concatenate([high, low], axis=0), mats[level, 0:rank],
                       preferred_element_type=jnp.float32)
        rest = jnp.dot(high, mats[level, rank:2 * rank], preferred_element_type=jnp.float32)
        terms = both[:size] + both[size:] + rest
        sent[level, rows] = terms[:, rank:]
        exchange(level, k, rows).start()
        own[rows] = terms[:, :rank]

    def finish(size, k, row):
        rows = pl.ds(pl.multiple_of(row, 16), size)
        exchange(levels - 1, k, rows).wait_recv()
        own[rows] = own[rows] + got[levels, rows]

        @pl.when(lax.rem(row + size, LANES) == 0)
        def _():
            b = lax.div(row, LANES)
            back[b] = own[pl.ds(pl.multiple_of(b * LANES, LANES), LANES)].T
            store_block(b).start()

    pl.semaphore_wait(barrier, min(bits, levels))

    pack = 1
    while (base * base) ** (pack + 1) < 2**31:
        pack += 1
    digits = [level * base + k for level, k in order]
    words = [
        sum(d * (base * base) ** i for i, d in enumerate(digits[n:n + pack]))
        for n in range(0, len(digits), pack)
    ]
    per = GROUP // pack
    groups = pl.cdiv(len(words), per)
    words += [0] * (groups * per - len(words))

    def group(g, carry):
        held = []
        for n in range(per):
            word = jnp.int32(words[n])
            for other in range(1, groups):
                word = jnp.where(g == other, jnp.int32(words[other * per + n]), word)
            held.append(word)

        def step(j, carry):
            word = held[0]
            for n in range(1, per):
                word = jnp.where(j >= n * pack, held[n], word)
            place = lax.rem(j, jnp.int32(pack))
            for i in range(1, pack):
                word = jnp.where(place >= i, lax.div(word, jnp.int32(base * base)), word)
            word = lax.rem(word, jnp.int32(base * base))
            level = lax.div(word, jnp.int32(base))
            k = lax.rem(word, jnp.int32(base))
            row = jnp.int32(0)
            for first, column, size in runs:
                row = jnp.where(k >= first, column + (k - first) * size, row)

            for n, size in enumerate(sorted(set(sizes))):
                among = False
                for (first, _, its), last in zip(runs, [r[0] for r in runs[1:]] + [len(sizes)]):
                    if its == size:
                        among = among | ((k >= first) & (k < last))

                @pl.when(among & (level < levels))
                def _():
                    apply(size, level, k, row)

                @pl.when(among & (level == levels))
                def _():
                    finish(size, k, row)
            return carry

        count = jnp.minimum(per * pack, len(order) - g * per * pack)
        return lax.fori_loop(0, count, step, carry)

    lax.fori_loop(0, groups, group, 0)

    for level in range(levels):
        exchange(level, 0, pl.ds(0, cols)).wait_send()

    for b in range(blocks):
        store_block(b).wait()


def on_device(coeffs, transfers):
    bits = lax.axis_size("bfly").bit_length() - 1
    _, rank, cols = coeffs.shape
    levels = transfers.shape[1]
    _, sizes = chunk_runs(cols)
    blocks = cols // LANES
    f32, bf16 = jnp.float32, jnp.bfloat16
    return pl.pallas_call(
        functools.partial(kernel, "bfly", bits, levels),
        out_shape=jax.ShapeDtypeStruct(coeffs.shape, f32),
        in_specs=[pl.BlockSpec(memory_space=pl.ANY)] * 2,
        out_specs=pl.BlockSpec(memory_space=pl.ANY),
        scratch_shapes=[
            pltpu.VMEM((cols, rank), f32),
            pltpu.VMEM((levels, cols, rank), f32),
            pltpu.VMEM((levels + 1, cols, rank), f32),
            pltpu.VMEM((levels, 2, rank, rank), f32),
            pltpu.VMEM((levels, 2 * rank, 2 * rank), bf16),
            pltpu.VMEM((blocks, rank, LANES), f32),
            pltpu.VMEM((blocks, rank, LANES), f32),
            pltpu.SemaphoreType.DMA((blocks,)),
            pltpu.SemaphoreType.DMA((levels,)),
            pltpu.SemaphoreType.DMA((blocks,)),
            pltpu.SemaphoreType.DMA((levels,)),
            pltpu.SemaphoreType.DMA((levels, len(sizes))),
        ],
        compiler_params=pltpu.CompilerParams(
            collective_id=0, has_side_effects=True, vmem_limit_bytes=60 * 2**20
        ),
        name="butterfly",
    )(coeffs, transfers)


def solution(mesh):
    return jax.shard_map(
        on_device,
        mesh=mesh,
        in_specs=(P("bfly", None, None), P("bfly", None, None, None, None)),
        out_specs=P("bfly", None, None),
        check_vma=False,
    )
```

profile of v0, /device:TPU:0, one launch (start us, length us, event | category | flops | bytes accessed | tf_op | source)
XLA Modules:
  0.0 107.2 jit_solution(17145836783890038922)
XLA Ops:
  0.0 104.4 %butterfly.1 = f32[1,384,1024]{2,1,0:T(8,128)} custom-call(f32[1,384,1024]{2,1,0:T(8,128)} %coeffs.1, f32[1,8,2,384,384]{4,3,2,1,0:T(8,128)} %transfers.1), custom_call_target="tpu_custom_call" | custom-call | tf_op jit(solution)/shard_map/butterfly/pallas_call | solution.py:208
  104.5 2.7 %copy.4 = f32[1,384,1024]{2,1,0:T(8,128)} copy(f32[1,384,1024]{2,1,0:T(8,128)} %butterfly.1) | data formatting | bytes 3145728
where the time goes:
time: 107 us
  Pallas kernels  104 us (97%)
  local copies, waits for them, and re-layouts  2.73 us (3%)
    pallas_call x1, Pallas kernels, on_device(): pl.pallas_call(functools.partial(kernel, 'bfly', bits, levels), out_shape...  104 us
    unnamed x1, local copies, waits for them, and re-layouts  2.73 us

commit v1 on v0

--- a/solution.py
+++ b/solution.py
@@ -10,9 +10,12 @@
 LANES = 128
 CHUNK = 64
 RAMP = (32, 32)
-DUE = (0.0, 2.1, 6.5, 11.9, 17.4, 24.8, 25.6, 33.5, 44.4)
+DUE = (0.0, 4.3, 9.0, 13.5, 18.0, 25.0, 27.5, 33.5, 42.0)
 PACE = 0.066
+AHEAD = 0.066
+TURN = 4
 GROUP = 9
+PREPARE_AFTER = 2
 
 
 def chunk_runs(cols):
@@ -29,21 +32,47 @@
 
 def task_order(sizes, levels):
     dues = [DUE[i] if i < len(DUE) else DUE[-1] + 6.0 * (i - len(DUE) + 1) for i in range(levels + 1)]
-    steps = sorted(
-        (sum(sizes[:k]) * PACE + dues[level], -level, level, k)
+    firsts = [sum(sizes[:k]) for k in range(len(sizes))]
+    steps = [
+        (firsts[k] * (AHEAD if level < TURN else PACE) + dues[level], -level, level, k)
         for k in range(len(sizes)) for level in range(levels + 1)
-    )
-    return [(level, k) for _, _, level, k in steps]
-
-
-def kernel(axis, bits, levels, coeffs, transfers, out, own, sent, got, raw, mats, turn, back,
-           in_sem, raw_sem, out_sem, send_sem, recv_sem):
+    ]
+    order, turned = [], {0}
+    for _, _, level, k in sorted(steps):
+        block = firsts[k] // LANES
+        if level == 0 and block not in turned:
+            turned.add(block)
+            order.append((levels + 2, block))
+        order.append((level, k))
+    for level in range(1, levels):
+        at = order.index((level - 1, min(PREPARE_AFTER, len(sizes) - 1)))
+        order.insert(min(at + 1, order.index((level, 0))), (levels + 1, level))
+    return order
+
+
+def ring_size(order, sizes, levels):
+    place = {task: i for i, task in enumerate(order)}
+    for ring in range(1, len(sizes)):
+        if all(
+            any(
+                place[level + 1, k] < place[level, j] and place[level + 1, j] < place[level, k + ring]
+                for j in range(len(sizes))
+            )
+            for level in range(levels) for k in range(len(sizes) - ring)
+        ):
+            return ring
+    return len(sizes)
+
+
+def kernel(axis, bits, levels, coeffs, transfers, out, own, sent, got, raw, mats, turn,
+           in_sem, raw_sem, send_sem, recv_sem):
     me = lax.axis_index(axis)
     cols, rank = own.shape
     blocks = cols // LANES
     runs, sizes = chunk_runs(cols)
     order = task_order(sizes, levels)
-    base = max(levels + 1, len(sizes))
+    base = max(levels + 3, len(sizes))
+    ring = ring_size(order, sizes, levels)
 
     def peer(level):
         step = lax.shift_left(jnp.int32(1), lax.rem(jnp.int32(level), jnp.int32(bits)))
@@ -52,21 +81,28 @@
     def lanes(b):
         return pl.ds(pl.multiple_of(b * LANES, LANES), LANES)
 
-    def load_block(b):
-        return pltpu.make_async_copy(coeffs.at[0, :, lanes(b)], turn.at[b], in_sem.at[b])
-
-    def load_level(level):
-        return pltpu.make_async_copy(transfers.at[0, level], raw.at[level], raw_sem.at[level])
-
-    def store_block(b):
-        return pltpu.make_async_copy(back.at[b], out.at[0, :, lanes(b)], out_sem.at[b])
+    def load_columns(first, count, sem):
+        columns = (slice(None), pl.ds(first, count))
+        return pltpu.make_async_copy(coeffs.at[(0, *columns)], turn.at[columns], in_sem.at[sem])
+
+    def load_side(side):
+        return pltpu.make_async_copy(transfers.at[0, 0, side], raw.at[0, side], raw_sem.at[side])
+
+    def load_levels(first, count, sem):
+        those = pl.ds(first, count)
+        return pltpu.make_async_copy(transfers.at[0, those], raw.at[those], raw_sem.at[sem])
+
+    loads = [load_columns(0, LANES, 0)]
+    if blocks > 1:
+        loads.append(load_columns(LANES, cols - LANES, 1))
+    later = [load_levels(1, 1, 2), load_levels(2, levels - 2, 3)]
 
     def exchange(level, k, rows):
         return pltpu.make_async_remote_copy(
             src_ref=sent.at[level, rows],
             dst_ref=got.at[level + 1, rows],
-            send_sem=send_sem.at[level],
-            recv_sem=recv_sem.at[level, k],
+            send_sem=send_sem.at[0],
+            recv_sem=recv_sem.at[level * ring + lax.rem(k, ring)],
             device_id=(peer(level),),
             device_id_type=pl.DeviceIdType.MESH,
         )
@@ -76,38 +112,37 @@
         pl.semaphore_signal(barrier, inc=1, device_id=(peer(bit),),
                             device_id_type=pl.DeviceIdType.MESH)
 
-    load_block(0).start()
-    for level in range(levels):
-        load_level(level).start()
-        if level == 0:
-            for b in range(1, blocks):
-                load_block(b).start()
+    load_side(1).start()
+    loads[0].start()
+    load_side(0).start()
+    later[0].start()
+    for load in loads[1:]:
+        load.start()
+    later[1].start()
+
+    def prepare_side(level, side):
+        full = raw[level, side].T
+        high = full.astype(jnp.bfloat16)
+        low = (full - high.astype(jnp.float32)).astype(jnp.bfloat16)
+        mats[level, 0:rank, side * rank:(side + 1) * rank] = high
+        mats[level, rank:2 * rank, side * rank:(side + 1) * rank] = low
 
     def prepare(level):
-        load_level(level).wait()
+        for n, load in enumerate(later):
+            @pl.when(level == n + 1)
+            def _():
+                load.wait()
+
         for side in range(2):
-            full = raw[level, side].T
-            high = full.astype(jnp.bfloat16)
-            low = (full - high.astype(jnp.float32)).astype(jnp.bfloat16)
-            mats[level, 0:rank, side * rank:(side + 1) * rank] = high
-            mats[level, rank:2 * rank, side * rank:(side + 1) * rank] = low
+            prepare_side(level, side)
 
     def turn_block(b):
-        load_block(b).wait()
         rows = pl.ds(pl.multiple_of(b * LANES, LANES), LANES)
-        own[rows] = turn[b].T
+        own[rows] = turn[:, rows].T
         got[0, rows] = jnp.zeros((LANES, rank), jnp.float32)
 
     def apply(size, level, k, row):
         rows = pl.ds(pl.multiple_of(row, 16), size)
-
-        @pl.when(k == 0)
-        def _():
-            prepare(level)
-
-        @pl.when((level == 0) & (lax.rem(row, LANES) == 0))
-        def _():
-            turn_block(lax.div(row, LANES))
 
         @pl.when(level > 0)
         def _():
@@ -132,9 +167,14 @@
         @pl.when(lax.rem(row + size, LANES) == 0)
         def _():
             b = lax.div(row, LANES)
-            back[b] = own[pl.ds(pl.multiple_of(b * LANES, LANES), LANES)].T
-            store_block(b).start()
-
+            out[0, :, lanes(b)] = own[pl.ds(pl.multiple_of(b * LANES, LANES), LANES)].T
+
+    load_side(1).wait()
+    prepare_side(0, 1)
+    loads[0].wait()
+    turn_block(0)
+    load_side(0).wait()
+    prepare_side(0, 0)
     pl.semaphore_wait(barrier, min(bits, levels))
 
     pack = 1
@@ -184,6 +224,18 @@
                 @pl.when(among & (level == levels))
                 def _():
                     finish(size, k, row)
+
+            @pl.when(level == levels + 1)
+            def _():
+                prepare(k)
+
+            @pl.when(level == levels + 2)
+            def _():
+                @pl.when(k == 1)
+                def _():
+                    loads[1].wait()
+
+                turn_block(k)
             return carry
 
         count = jnp.minimum(per * pack, len(order) - g * per * pack)
@@ -191,11 +243,10 @@
 
     lax.fori_loop(0, groups, group, 0)
 
-    for level in range(levels):
-        exchange(level, 0, pl.ds(0, cols)).wait_send()
-
-    for b in range(blocks):
-        store_block(b).wait()
+    pltpu.make_async_remote_copy(
+        src_ref=sent, dst_ref=got.at[pl.ds(1, levels)], send_sem=send_sem.at[0], recv_sem=recv_sem.at[0],
+        device_id=(peer(0),), device_id_type=pl.DeviceIdType.MESH,
+    ).wait_send()
 
 
 def on_device(coeffs, transfers):
@@ -203,29 +254,26 @@
     _, rank, cols = coeffs.shape
     levels = transfers.shape[1]
     _, sizes = chunk_runs(cols)
-    blocks = cols // LANES
     f32, bf16 = jnp.float32, jnp.bfloat16
     return pl.pallas_call(
         functools.partial(kernel, "bfly", bits, levels),
-        out_shape=jax.ShapeDtypeStruct(coeffs.shape, f32),
+        out_shape=pltpu.VMEM(coeffs.shape, f32),
         in_specs=[pl.BlockSpec(memory_space=pl.ANY)] * 2,
-        out_specs=pl.BlockSpec(memory_space=pl.ANY),
+        out_specs=pl.BlockSpec(memory_space=pltpu.VMEM),
         scratch_shapes=[
             pltpu.VMEM((cols, rank), f32),
             pltpu.VMEM((levels, cols, rank), f32),
             pltpu.VMEM((levels + 1, cols, rank), f32),
             pltpu.VMEM((levels, 2, rank, rank), f32),
             pltpu.VMEM((levels, 2 * rank, 2 * rank), bf16),
-            pltpu.VMEM((blocks, rank, LANES), f32),
-            pltpu.VMEM((blocks, rank, LANES), f32),
-            pltpu.SemaphoreType.DMA((blocks,)),
-            pltpu.SemaphoreType.DMA((levels,)),
-            pltpu.SemaphoreType.DMA((blocks,)),
-            pltpu.SemaphoreType.DMA((levels,)),
-            pltpu.SemaphoreType.DMA((levels, len(sizes))),
+            pltpu.VMEM((rank, cols), f32),
+            pltpu.SemaphoreType.DMA((2,)),
+            pltpu.SemaphoreType.DMA((4,)),
+            pltpu.SemaphoreType.DMA((1,)),
+            pltpu.SemaphoreType.DMA((levels * ring_size(task_order(sizes, levels), sizes, levels),)),
         ],
         compiler_params=pltpu.CompilerParams(
-            collective_id=0, has_side_effects=True, vmem_limit_bytes=60 * 2**20
+            collective_id=0, has_side_effects=True, vmem_limit_bytes=52 * 2**20
         ),
         name="butterfly",
     )(coeffs, transfers)

time: 107 us -> 104 us (0.972)
  local copies, waits for them, and re-layouts: 2.73 us -> 1.15 us
    pallas_call x1, Pallas kernels: 104 us -> 103 us  [on_device(): pl.pallas_call(functools.partial(kernel, 'bfly', bits, levels), out_shape...]
    unnamed x1, local copies, waits for them, and re-layouts: 2.73 us -> 1.15 us
where the time goes in v1:
time: 104 us
  Pallas kernels  103 us (99%)
  local copies, waits for them, and re-layouts  1.15 us (1%)
    pallas_call x1, Pallas kernels, on_device(): pl.pallas_call(functools.partial(kernel, 'bfly', bits, levels), out_shape...  103 us

profile of v1, /device:TPU:0, one launch (start us, length us, event | category | flops | bytes accessed | tf_op | source)
XLA Modules:
  0.0 103.7 jit_solution(9486531698556495934)
XLA Ops:
  0.0 102.5 %butterfly.1 = f32[1,384,1024]{2,1,0:T(8,128)S(1)} custom-call(f32[1,384,1024]{2,1,0:T(8,128)} %coeffs.1, f32[1,8,2,384,384]{4,3,2,1,0:T(8,128)} %transfers.1), custom_call_target="tpu_custom_call" | custom-call | tf_op jit(solution)/shard_map/butterfly/pallas_call | solution.py:258
  102.5 1.1 %copy.4 = f32[1,384,1024]{2,1,0:T(8,128)} copy(f32[1,384,1024]{2,1,0:T(8,128)S(1)} %butterfly.1) | data formatting | bytes 3145728

commit v2 on v1

--- a/solution.py
+++ b/solution.py
@@ -9,13 +9,13 @@
 
 LANES = 128
 CHUNK = 64
-RAMP = (32, 32)
-DUE = (0.0, 4.3, 9.0, 13.5, 18.0, 25.0, 27.5, 33.5, 42.0)
-PACE = 0.066
-AHEAD = 0.066
+RAMP = (32, 32, 32, 32,)
+DUE = (0.00, 3.90, 11.33, 18.99, 26.21, 37.55, 40.12, 48.33, 59.96)
+PACE = 0.0716
+AHEAD = 0.0700
 TURN = 4
 GROUP = 9
-PREPARE_AFTER = 2
+PREPARE_AFTER = 4
 
 
 def chunk_runs(cols):
@@ -45,9 +45,13 @@
             order.append((levels + 2, block))
         order.append((level, k))
     for level in range(1, levels):
-        at = order.index((level - 1, min(PREPARE_AFTER, len(sizes) - 1)))
+        at = order.index((level - 1, min(PREPARE_AFTER if level > 1 else 0, len(sizes) - 1)))
         order.insert(min(at + 1, order.index((level, 0))), (levels + 1, level))
     return order
+
+
+def modulo(x, n):
+    return lax.bitwise_and(x, jnp.int32(n - 1)) if n & (n - 1) == 0 else lax.rem(x, jnp.int32(n))
 
 
 def ring_size(order, sizes, levels):
@@ -60,7 +64,7 @@
             )
             for level in range(levels) for k in range(len(sizes) - ring)
         ):
-            return ring
+            return 8 if ring in (5, 6, 7) else ring
     return len(sizes)
 
 
@@ -71,12 +75,13 @@
     blocks = cols // LANES
     runs, sizes = chunk_runs(cols)
     order = task_order(sizes, levels)
-    base = max(levels + 3, len(sizes))
     ring = ring_size(order, sizes, levels)
 
     def peer(level):
-        step = lax.shift_left(jnp.int32(1), lax.rem(jnp.int32(level), jnp.int32(bits)))
-        return me + step * (1 - 2 * lax.rem(lax.div(me, step), jnp.int32(2)))
+        bit = jnp.int32(level)
+        for _ in range((levels - 1) // bits):
+            bit = jnp.where(bit >= bits, bit - bits, bit)
+        return lax.bitwise_xor(me, lax.shift_left(jnp.int32(1), bit))
 
     def lanes(b):
         return pl.ds(pl.multiple_of(b * LANES, LANES), LANES)
@@ -102,7 +107,7 @@
             src_ref=sent.at[level, rows],
             dst_ref=got.at[level + 1, rows],
             send_sem=send_sem.at[0],
-            recv_sem=recv_sem.at[level * ring + lax.rem(k, ring)],
+            recv_sem=recv_sem.at[level * ring + modulo(k, ring)],
             device_id=(peer(level),),
             device_id_type=pl.DeviceIdType.MESH,
         )
@@ -141,6 +146,20 @@
         own[rows] = turn[:, rows].T
         got[0, rows] = jnp.zeros((LANES, rank), jnp.float32)
 
+    def products(state, level):
+        size = state.shape[0]
+        high = state.astype(jnp.bfloat16)
+        low = (state - high.astype(jnp.float32)).astype(jnp.bfloat16)
+        stack = jnp.concatenate([high, low], axis=0)
+
+        def terms(first, count):
+            columns = slice(first * rank, (first + count) * rank)
+            both = jnp.dot(stack, mats[level, 0:rank, columns], preferred_element_type=jnp.float32)
+            rest = jnp.dot(high, mats[level, rank:2 * rank, columns], preferred_element_type=jnp.float32)
+            return both[:size] + both[size:] + rest
+
+        return terms
+
     def apply(size, level, k, row):
         rows = pl.ds(pl.multiple_of(row, 16), size)
 
@@ -148,16 +167,16 @@
         def _():
             exchange(level - 1, k, rows).wait_recv()
 
-        state = own[rows] + got[level, rows]
-        high = state.astype(jnp.bfloat16)
-        low = (state - high.astype(jnp.float32)).astype(jnp.bfloat16)
-        both = jnp.dot(jnp.concatenate([high, low], axis=0), mats[level, 0:rank],
-                       preferred_element_type=jnp.float32)
-        rest = jnp.dot(high, mats[level, rank:2 * rank], preferred_element_type=jnp.float32)
-        terms = both[:size] + both[size:] + rest
-        sent[level, rows] = terms[:, rank:]
-        exchange(level, k, rows).start()
-        own[rows] = terms[:, :rank]
+        terms = products(own[rows] + got[level, rows], level)
+        if size < CHUNK:
+            sent[level, rows] = terms(1, 1)
+            exchange(level, k, rows).start()
+            own[rows] = terms(0, 1)
+        else:
+            both = terms(0, 2)
+            sent[level, rows] = both[:, rank:]
+            exchange(level, k, rows).start()
+            own[rows] = both[:, :rank]
 
     def finish(size, k, row):
         rows = pl.ds(pl.multiple_of(row, 16), size)
@@ -173,16 +192,21 @@
     prepare_side(0, 1)
     loads[0].wait()
     turn_block(0)
+    pl.semaphore_wait(barrier, min(bits, levels))
+
+    rows = pl.ds(0, sizes[0])
+    terms = products(own[rows], 0)
+    sent[0, rows] = terms(1, 1)
+    exchange(jnp.int32(0), jnp.int32(0), rows).start()
     load_side(0).wait()
     prepare_side(0, 0)
-    pl.semaphore_wait(barrier, min(bits, levels))
-
-    pack = 1
-    while (base * base) ** (pack + 1) < 2**31:
-        pack += 1
-    digits = [level * base + k for level, k in order]
+    own[rows] = terms(0, 1)
+
+    width = max(levels + 2, len(sizes) - 1).bit_length()
+    pack = 31 // (2 * width)
+    digits = [(level << width) + k for level, k in order if (level, k) != (0, 0)]
     words = [
-        sum(d * (base * base) ** i for i, d in enumerate(digits[n:n + pack]))
+        sum(d << (2 * width * i) for i, d in enumerate(digits[n:n + pack]))
         for n in range(0, len(digits), pack)
     ]
     per = GROUP // pack
@@ -201,29 +225,34 @@
             word = held[0]
             for n in range(1, per):
                 word = jnp.where(j >= n * pack, held[n], word)
-            place = lax.rem(j, jnp.int32(pack))
-            for i in range(1, pack):
-                word = jnp.where(place >= i, lax.div(word, jnp.int32(base * base)), word)
-            word = lax.rem(word, jnp.int32(base * base))
-            level = lax.div(word, jnp.int32(base))
-            k = lax.rem(word, jnp.int32(base))
+            place = j
+            for n in range(1, per):
+                place = jnp.where(j >= n * pack, j - n * pack, place)
+            word = lax.shift_right_logical(word, place * (2 * width))
+            level = lax.bitwise_and(lax.shift_right_logical(word, jnp.int32(width)), jnp.int32(2**width - 1))
+            k = lax.bitwise_and(word, jnp.int32(2**width - 1))
             row = jnp.int32(0)
             for first, column, size in runs:
                 row = jnp.where(k >= first, column + (k - first) * size, row)
 
-            for n, size in enumerate(sorted(set(sizes))):
-                among = False
-                for (first, _, its), last in zip(runs, [r[0] for r in runs[1:]] + [len(sizes)]):
-                    if its == size:
-                        among = among | ((k >= first) & (k < last))
-
-                @pl.when(among & (level < levels))
-                def _():
-                    apply(size, level, k, row)
-
-                @pl.when(among & (level == levels))
-                def _():
-                    finish(size, k, row)
+            def by_size(act):
+                for size in sorted(set(sizes)):
+                    among = False
+                    for (first, _, its), last in zip(runs, [r[0] for r in runs[1:]] + [len(sizes)]):
+                        if its == size:
+                            among = among | ((k >= first) & (k < last))
+
+                    @pl.when(among)
+                    def _():
+                        act(size)
+
+            @pl.when(level < levels)
+            def _():
+                by_size(lambda size: apply(size, level, k, row))
+
+            @pl.when(level == levels)
+            def _():
+                by_size(lambda size: finish(size, k, row))
 
             @pl.when(level == levels + 1)
             def _():
@@ -238,7 +267,7 @@
                 turn_block(k)
             return carry
 
-        count = jnp.minimum(per * pack, len(order) - g * per * pack)
+        count = jnp.minimum(per * pack, len(digits) - g * per * pack)
         return lax.fori_loop(0, count, step, carry)
 
     lax.fori_loop(0, groups, group, 0)

time: 104 us -> 100 us (0.962)
  Pallas kernels: 103 us -> 98.8 us
    pallas_call x1, Pallas kernels: 103 us -> 98.8 us  [on_device(): pl.pallas_call(functools.partial(kernel, 'bfly', bits, levels), out_shape...]
where the time goes in v2:
time: 100 us
  Pallas kernels  98.8 us (99%)
  local copies, waits for them, and re-layouts  1.15 us (1%)
    pallas_call x1, Pallas kernels, on_device(): pl.pallas_call(functools.partial(kernel, 'bfly', bits, levels), out_shape...  98.8 us

profile of v2, /device:TPU:0, one launch (start us, length us, event | category | flops | bytes accessed | tf_op | source)
XLA Modules:
  0.0 100.0 jit_solution(11366128086151779237)
XLA Ops:
  0.0 98.8 %butterfly.1 = f32[1,384,1024]{2,1,0:T(8,128)S(1)} custom-call(f32[1,384,1024]{2,1,0:T(8,128)} %coeffs.1, f32[1,8,2,384,384]{4,3,2,1,0:T(8,128)} %transfers.1), custom_call_target="tpu_custom_call" | custom-call | tf_op jit(solution)/shard_map/butterfly/pallas_call | solution.py:287
  98.9 1.1 %copy.4 = f32[1,384,1024]{2,1,0:T(8,128)} copy(f32[1,384,1024]{2,1,0:T(8,128)S(1)} %butterfly.1) | data formatting | bytes 3145728

commit v3 on v2

--- a/solution.py
+++ b/solution.py
@@ -10,19 +10,22 @@
 LANES = 128
 CHUNK = 64
 RAMP = (32, 32, 32, 32,)
-DUE = (0.00, 3.90, 11.33, 18.99, 26.21, 37.55, 40.12, 48.33, 59.96)
-PACE = 0.0716
+TAIL = (32, 32, 32, 32,)
+DUE = (0.00, 3.90, 11.33, 18.92, 26.21, 35.99, 38.56, 47.12, 57.99)
+PACE = 0.0710
 AHEAD = 0.0700
 TURN = 4
 GROUP = 9
 PREPARE_AFTER = 4
+PREPARE_EARLY = {1: (0, 0), 2: (1, 1), 3: (1, 2), 4: (2, 1)}
+LEAD = 0.00
 
 
 def chunk_runs(cols):
-    body = cols - 2 * sum(RAMP)
+    body = cols - sum(RAMP) - sum(TAIL)
     sizes = (CHUNK,) * (cols // CHUNK)
     if body > 0 and body % CHUNK == 0:
-        sizes = RAMP + (CHUNK,) * (body // CHUNK) + RAMP[::-1]
+        sizes = RAMP + (CHUNK,) * (body // CHUNK) + TAIL
     runs = []
     for k, size in enumerate(sizes):
         if not runs or runs[-1][2] != size:
@@ -34,7 +37,7 @@
     dues = [DUE[i] if i < len(DUE) else DUE[-1] + 6.0 * (i - len(DUE) + 1) for i in range(levels + 1)]
     firsts = [sum(sizes[:k]) for k in range(len(sizes))]
     steps = [
-        (firsts[k] * (AHEAD if level < TURN else PACE) + dues[level], -level, level, k)
+        (firsts[k] * (AHEAD if level < TURN else PACE) + dues[level] - (LEAD if k == 0 else 0.0), -level, level, k)
         for k in range(len(sizes)) for level in range(levels + 1)
     ]
     order, turned = [], {0}
@@ -45,7 +48,8 @@
             order.append((levels + 2, block))
         order.append((level, k))
     for level in range(1, levels):
-        at = order.index((level - 1, min(PREPARE_AFTER if level > 1 else 0, len(sizes) - 1)))
+        after, k = PREPARE_EARLY.get(level, (level - 1, PREPARE_AFTER))
+        at = order.index((after, min(k, len(sizes) - 1)))
         order.insert(min(at + 1, order.index((level, 0))), (levels + 1, level))
     return order
 
@@ -168,15 +172,22 @@
             exchange(level - 1, k, rows).wait_recv()
 
         terms = products(own[rows] + got[level, rows], level)
-        if size < CHUNK:
-            sent[level, rows] = terms(1, 1)
-            exchange(level, k, rows).start()
-            own[rows] = terms(0, 1)
-        else:
+        def together():
             both = terms(0, 2)
             sent[level, rows] = both[:, rank:]
             exchange(level, k, rows).start()
             own[rows] = both[:, :rank]
+
+        def apart():
+            sent[level, rows] = terms(1, 1)
+            exchange(level, k, rows).start()
+            own[rows] = terms(0, 1)
+
+        if size in (sizes[0], sizes[-1]):
+            pl.when((k == 0) | (k == len(sizes) - 1))(apart)
+            pl.when((k > 0) & (k < len(sizes) - 1))(together)
+        else:
+            together()
 
     def finish(size, k, row):
         rows = pl.ds(pl.multiple_of(row, 16), size)

time: 100 us -> 99.5 us (level)
  no operation moved by 1% of the time
where the time goes in v3:
time: 99.5 us; the launch traced here: 99.3 us
  Pallas kernels  98.2 us (99%)
  local copies, waits for them, and re-layouts  1.15 us (1%)
    pallas_call x1, Pallas kernels, on_device(): pl.pallas_call(functools.partial(kernel, 'bfly', bits, levels), out_shape...  98.2 us

profile of v3, /device:TPU:0, one launch (start us, length us, event | category | flops | bytes accessed | tf_op | source)
XLA Modules:
  0.0 99.3 jit_solution(10616648141528360653)
XLA Ops:
  0.0 98.2 %butterfly.1 = f32[1,384,1024]{2,1,0:T(8,128)S(1)} custom-call(f32[1,384,1024]{2,1,0:T(8,128)} %coeffs.1, f32[1,8,2,384,384]{4,3,2,1,0:T(8,128)} %transfers.1), custom_call_target="tpu_custom_call" | custom-call | tf_op jit(solution)/shard_map/butterfly/pallas_call | solution.py:298
  98.2 1.1 %copy.4 = f32[1,384,1024]{2,1,0:T(8,128)} copy(f32[1,384,1024]{2,1,0:T(8,128)S(1)} %butterfly.1) | data formatting | bytes 3145728

commit v4 on v3

--- a/solution.py
+++ b/solution.py
@@ -16,7 +16,7 @@
 AHEAD = 0.0700
 TURN = 4
 GROUP = 9
-PREPARE_AFTER = 4
+PREPARE_AFTER = 2
 PREPARE_EARLY = {1: (0, 0), 2: (1, 1), 3: (1, 2), 4: (2, 1)}
 LEAD = 0.00
 

time: 99.5 us -> 99.5 us (level)
  no operation moved by 1% of the time
where the time goes in v4:
time: 99.5 us; the launch traced here: 99.3 us
  Pallas kernels  98.2 us (99%)
  local copies, waits for them, and re-layouts  1.15 us (1%)
    pallas_call x1, Pallas kernels, on_device(): pl.pallas_call(functools.partial(kernel, 'bfly', bits, levels), out_shape...  98.2 us

profile of v4, /device:TPU:0, one launch (start us, length us, event | category | flops | bytes accessed | tf_op | source)
XLA Modules:
  0.0 99.3 jit_solution(11341840532577877089)
XLA Ops:
  0.0 98.2 %butterfly.1 = f32[1,384,1024]{2,1,0:T(8,128)S(1)} custom-call(f32[1,384,1024]{2,1,0:T(8,128)} %coeffs.1, f32[1,8,2,384,384]{4,3,2,1,0:T(8,128)} %transfers.1), custom_call_target="tpu_custom_call" | custom-call | tf_op jit(solution)/shard_map/butterfly/pallas_call | solution.py:298
  98.2 1.1 %copy.4 = f32[1,384,1024]{2,1,0:T(8,128)} copy(f32[1,384,1024]{2,1,0:T(8,128)S(1)} %butterfly.1) | data formatting | bytes 3145728

commit v5 on v4

--- a/solution.py
+++ b/solution.py
@@ -17,7 +17,7 @@
 TURN = 4
 GROUP = 9
 PREPARE_AFTER = 2
-PREPARE_EARLY = {1: (0, 0), 2: (1, 1), 3: (1, 2), 4: (2, 1)}
+PREPARE_EARLY = {1: (0, 0), 2: (1, 1), 3: (1, 2), 4: (2, 2)}
 LEAD = 0.00
 
 

time: 99.5 us -> 99.5 us (level)
  no operation moved by 1% of the time
where the time goes in v5:
time: 99.5 us; the launch traced here: 99.3 us
  Pallas kernels  98.2 us (99%)
  local copies, waits for them, and re-layouts  1.15 us (1%)
    pallas_call x1, Pallas kernels, on_device(): pl.pallas_call(functools.partial(kernel, 'bfly', bits, levels), out_shape...  98.2 us

profile of v5, /device:TPU:0, one launch (start us, length us, event | category | flops | bytes accessed | tf_op | source)
XLA Modules:
  0.0 99.3 jit_solution(9184429012862741030)
XLA Ops:
  0.0 98.2 %butterfly.1 = f32[1,384,1024]{2,1,0:T(8,128)S(1)} custom-call(f32[1,384,1024]{2,1,0:T(8,128)} %coeffs.1, f32[1,8,2,384,384]{4,3,2,1,0:T(8,128)} %transfers.1), custom_call_target="tpu_custom_call" | custom-call | tf_op jit(solution)/shard_map/butterfly/pallas_call | solution.py:298
  98.2 1.1 %copy.4 = f32[1,384,1024]{2,1,0:T(8,128)} copy(f32[1,384,1024]{2,1,0:T(8,128)S(1)} %butterfly.1) | data formatting | bytes 3145728
